TPU v7x, 256 devices: a whole 4x4x8 slice. The times are simulated.
256 devices in a mesh: block: 16 (over z_hi, y), tok: 16 (over z_lo, x, core).
Axes of the slice: x: 4, y: 4, z: 8 (z_hi: 4, z_lo: 2; z = z_hi * 2 + z_lo), core: 2. Of those that a mesh axis runs over, the one named last changes fastest.
Arguments:
- queries: bfloat16 [262144, 512], P(('block', 'tok')), may hold values from -6 to 6
- keys: bfloat16 [262144, 512], P(('block', 'tok')), may hold values from -6 to 6
- values: bfloat16 [262144, 512], P(('block', 'tok')), may hold values from -6 to 6
- rates: float32 [3, 262144], P(None, ('block', 'tok')), may hold values from 0.3 to 3
- fast0: float32 [3, 512, 512], replicated, may hold values from -1 to 1
Outputs:
- outputs: bfloat16 [262144, 512], P(('block', 'tok'))
All inputs are finite; a program needn't handle non-finite values.
Results may differ from a plain program's by a relative error of at most 0.039.
Values may be sent and summed in bfloat16 or wider, within the bound.
No kernel may reach another device: no remote copies, remote signals or barrier semaphores. Data moves between devices by JAX's collectives and lax.ppermute only.
A program may use at most 128 MiB of HBM per device.

v0:
```python
import jax
import jax.numpy as jnp
from jax import lax
from jax.sharding import PartitionSpec as P


def carried_in(value, axis, join, neutral):
    place = lax.axis_index(axis)
    gathered = lax.all_gather(value.astype(jnp.bfloat16), axis)
    state = jnp.zeros_like(value) + jnp.asarray(neutral, value.dtype)

    def one(step, state):
        return join(state, lax.dynamic_index_in_dim(gathered, step, 0, False).astype(value.dtype))

    return lax.fori_loop(0, place, one, state)


def contract_cols(left, right):
    return lax.dot_general(
        left, right, (((1,), (1,)), ((), ())), preferred_element_type=jnp.float32
    )


def contract_rows(left, right):
    return lax.dot_general(
        left, right, (((0,), (0,)), ((), ())), preferred_element_type=jnp.float32
    )


def rescale(rows, target):
    return rows * (target / jnp.sqrt(jnp.sum(rows * rows, -1, keepdims=True) + 1e-06))


def fast_grads(weight_bf, keys, values, rates, scale):
    gate = contract_cols(keys, weight_bf[0])
    upper = contract_cols(keys, weight_bf[1])
    sigma = jax.nn.sigmoid(gate)
    active = gate * sigma
    hidden = active * upper
    back = -contract_cols(values, weight_bf[2])
    dgate = back * upper * sigma * (1.0 + gate * (1.0 - sigma))
    dupper = back * active
    rate = rates * scale
    grad_gate = contract_rows((rate[0][:, None] * dgate).astype(jnp.bfloat16), keys)
    grad_up = contract_rows((rate[1][:, None] * dupper).astype(jnp.bfloat16), keys)
    grad_down = -contract_rows((rate[2][:, None] * hidden).astype(jnp.bfloat16), values)
    return jnp.stack([grad_gate, grad_up, grad_down])


def apply_fast(weight_bf, queries):
    gate = contract_cols(queries, weight_bf[0])
    upper = contract_cols(queries, weight_bf[1])
    hidden = (jax.nn.silu(gate) * upper).astype(jnp.bfloat16)
    return jnp.dot(hidden, weight_bf[2], preferred_element_type=jnp.float32).astype(jnp.bfloat16)


def add_terms(earlier, later):
    return earlier + later


def shards(queries, keys, values, rates, fast0):
    groups = lax.axis_size("tok")
    scale = (keys.shape[0] * groups * keys.shape[1]) ** (-0.5)
    target = jnp.sqrt(jnp.sum(fast0 * fast0, -1, keepdims=True))
    weights = fast0
    for update_step in range(2):
        partial_grad = fast_grads(weights.astype(jnp.bfloat16), keys, values, rates, scale)
        total = lax.psum(partial_grad.astype(jnp.bfloat16), "tok").astype(jnp.float32)
        weights = rescale(weights - total, target)
    change = weights - fast0
    earlier = carried_in(change, "block", add_terms, jnp.zeros_like(change))
    applied = rescale(fast0 + (earlier + change), target).astype(jnp.bfloat16)
    return apply_fast(applied, queries)


def solution(mesh):
    return jax.shard_map(
        shards,
        mesh=mesh,
        in_specs=(
            P(("block", "tok"), None),
            P(("block", "tok"), None),
            P(("block", "tok"), None),
            P(None, ("block", "tok")),
            P(),
        ),
        out_specs=P(("block", "tok"), None),
        check_vma=False,
    )
```

profile of v0, /device:TPU:248, one launch (start us, length us, event | category | flops | bytes accessed | tf_op | source)
XLA Modules:
  0.0 626.2 jit_solution(16234509022687132216)
XLA Ops:
  6.5 0.0 copy-start
  6.5 0.0 all-reduce.3.cloned.1.call-start
  6.5 2.2 convert_element_type.50
  8.7 0.0 copy-done
  8.7 0.7 fusion.38
  9.5 0.0 copy-start.9
  9.5 0.0 copy-start.7
  9.5 0.7 fusion.39
  10.2 0.0 copy-done.9
  10.3 0.4 copy-done.7
  10.7 0.7 fusion.40
  11.5 1.2 fusion.21
  12.7 1.4 fusion.20
  14.1 1.1 fusion.25
  15.3 1.3 pad_maximum_fusion
  16.6 0.0 all-reduce.3.cloned.1.call-update
  16.6 0.0 all-reduce.5.cloned.1.call-start
  16.7 126.4 %all-reduce.3.cloned.1.call-done = bf16[3,512,512]{2,1,0:T(8,128)(2,1)} async-done(((bf16[3,512,512]{2,1,0:T(8,128)(2,1)}), bf16[3,512,512]{2,1,0:T(8,128)(2,1)}) %all-reduce.3.cloned.1.call-update) | async-done | bytes 1572880 | tf_op jit(solution)/shard_map/psum | solution.py:68
  143.0 3.2 multiply_reduce_fusion.3
  146.2 0.1 copy-done.2
  146.3 0.5 copy-done.4
  146.8 0.4 multiply_convert_fusion.1
  147.2 0.7 fusion.35
  147.9 0.7 fusion.36
  148.7 0.7 fusion.37
  149.4 1.1 fusion.24
  150.6 1.4 fusion.22
  152.0 1.2 fusion.23
  153.2 0.0 copy-start.3
  153.2 1.3 pad_maximum_fusion.1
  154.6 0.0 all-reduce.5.cloned.1.call-update
  154.6 0.2 all-gather.3.cloned.1.call-start
  154.8 127.2 %all-reduce.5.cloned.1.call-done = bf16[3,512,512]{2,1,0:T(8,128)(2,1)} async-done(((bf16[3,512,512]{2,1,0:T(8,128)(2,1)}), bf16[3,512,512]{2,1,0:T(8,128)(2,1)}) %all-reduce.5.cloned.1.call-update) | async-done | bytes 1572880 | tf_op jit(solution)/shard_map/psum | solution.py:68
  282.1 0.0 copy-done.3
  282.1 3.0 multiply_reduce_fusion.1
  285.1 0.0 copy-done.5
  285.1 0.0 copy-done.6
  285.1 1.8 fusion
  286.9 0.0 all-gather.3.cloned.1.call-update
  286.9 288.4 %all-gather.3.cloned.1.call-done = bf16[48,512,512]{2,1,0:T(8,128)(2,1)} async-done(((bf16[3,512,512]{2,1,0:T(8,128)(2,1)}), bf16[48,512,512]{2,1,0:T(8,128)(2,1)}) %all-gather.3.cloned.1.call-update) | async-done | bytes 25165840 | tf_op jit(solution)/shard_map/all_gather | solution.py:9
  575.3 0.4 broadcast_in_dim.2
  575.7 33.1 %while.10 = (s32[]{:T(128)}, f32[3,512,512]{2,1,0:T(8,128)S(1)}, s32[]{:T(128)}, bf16[16,3,512,512]{3,2,1,0:T(8,128)(2,1)}, s32[]{:T(128)}, /*index=5*/s32[]{:T(128)}, s32[]{:T(128)}) while((s32[]{:T(128)}, f32[3,512,512]{2,1,0:T(8,128)S(1)}, s32[]{:T(128)}, bf16[16,3,512,512]{3,2,1,0:T(8,128)(2,1)}, s32[]{:T(128)}, /*index=5*/s32[]{:T(128)}, ...), condition=%wide.region_6.7_spmd, body=%wide.region_5.6_spmd.sunk | while | flops 1572869 | bytes 7864443 | solution.py:15
  575.7 2.2 convert_add_fusion.2
  577.9 2.2 convert_add_fusion.2
  580.1 2.2 convert_add_fusion.2
  582.3 2.2 convert_add_fusion.2
  584.6 2.2 convert_add_fusion.2
  586.8 2.2 convert_add_fusion.2
  589.0 2.2 convert_add_fusion.2
  591.2 2.2 convert_add_fusion.2
  593.4 2.2 convert_add_fusion.2
  595.6 2.2 convert_add_fusion.2
  597.8 2.2 convert_add_fusion.2
  600.0 2.2 convert_add_fusion.2
  602.2 2.2 convert_add_fusion.2
  604.4 2.2 convert_add_fusion.2
  606.7 2.2 convert_add_fusion.2
  608.9 3.6 multiply_reduce_fusion
  612.5 0.0 copy-start.8
  612.5 1.4 multiply_convert_fusion
  614.0 1.8 fusion.34
  615.7 0.0 copy-start.1
  615.8 3.9 convolution_convert_fusion
  619.7 0.0 copy-done.1
  (10 shorter events, 0.1 us)
Async XLA Ops:
  6.5 2.2 copy-start
  6.5 136.5 %all-reduce.3.cloned.1.call-start = ((), (), s32[]{:S(2)}) async-start(), calls=%async_computation | async-start | bytes 3145728 | tf_op jit(solution)/shard_map/psum | solution.py:68
  9.5 0.8 copy-start.9
  9.5 1.2 copy-start.7
  16.6 265.4 %all-reduce.5.cloned.1.call-start = ((), (), s32[]{:S(2)}) async-start(), calls=%async_computation.1 | async-start | bytes 3145728 | tf_op jit(solution)/shard_map/psum | solution.py:68
  143.0 3.3 copy-start.2
  143.0 3.8 copy-start.4
  153.2 128.8 %copy-start.3 = (f32[3,512,512]{2,1,0:T(8,128)S(1)}, f32[3,512,512]{2,1,0:T(8,128)}, u32[]{:S(2)}) copy-start(f32[3,512,512]{2,1,0:T(8,128)} %param.11) | copy-start | bytes 9437188
  154.6 420.7 %all-gather.3.cloned.1.call-start = ((), (), s32[]{:S(2)}) async-start(), calls=%async_computation.2 | async-start | bytes 26738688 | tf_op jit(solution)/shard_map/all_gather | solution.py:9
  282.1 3.0 copy-start.5
  282.1 3.0 copy-start.6
  612.5 1.4 copy-start.8
  615.7 3.9 copy-start.1
Sparse Core Ops, SparseCore 0:
  16.7 126.2 all-reduce.2
  154.7 127.2 all-reduce.4
  287.0 288.2 all-gather.2
where the time goes:
time: 627 us; the launch traced here: 626 us
  waiting for transfers between devices  542 us (86%)
  other arithmetic  51.1 us (8%)
  matrix products  17.7 us (3%)
  between operations  13.3 us (2%)
    all_gather x1, waiting for transfers between devices, carried_in(): gathered = lax.all_gather(value.astype(jnp.bfloat16), axis)  288 us
    psum x2, waiting for transfers between devices, shards(): lax.psum(partial_grad.astype(jnp.bfloat16), 'tok').astype(jnp.float32)  254 us
    add x15, other arithmetic, add_terms(): return earlier + later  32.7 us
  transfers between devices with their start and end apart: 3, of which 3 were waited for; matrix products, arithmetic and copies ran while one was open for 0% of the time, Pallas kernels for 0%

commit v1 on v0

--- a/solution.py
+++ b/solution.py
@@ -1,7 +1,15 @@
+import functools
 import jax
 import jax.numpy as jnp
 from jax import lax
 from jax.sharding import PartitionSpec as P
+
+
+def _begin_quarters(local_values, ax_name):
+    return jax.lax.all_gather(local_values, ax_name).sum(axis=0)
+
+
+_supply_all_arrays = functools.partial(_begin_quarters, ax_name="tok")
 
 
 def carried_in(value, axis, join, neutral):
@@ -65,7 +73,7 @@
     weights = fast0
     for update_step in range(2):
         partial_grad = fast_grads(weights.astype(jnp.bfloat16), keys, values, rates, scale)
-        total = lax.psum(partial_grad.astype(jnp.bfloat16), "tok").astype(jnp.float32)
+        total = _supply_all_arrays(partial_grad.astype(jnp.bfloat16)).astype(jnp.float32)
         weights = rescale(weights - total, target)
     change = weights - fast0
     earlier = carried_in(change, "block", add_terms, jnp.zeros_like(change))

time: 627 us -> 668 us (1.065)
  other arithmetic: 51.1 us -> 77.6 us
  waiting for transfers between devices: 542 us -> 556 us
    all_gather x0 -> x2, waiting for transfers between devices: none -> 268 us  [_begin_quarters(): return jax.lax.all_gather(local_values, ax_name).sum(axis=0)]
    psum x2 -> x0, waiting for transfers between devices: 254 us -> none  [shards(): lax.psum(partial_grad.astype(jnp.bfloat16), 'tok').astype(jnp.float32)]
    reduce_sum x0 -> x2, other arithmetic: none -> 27.7 us  [_begin_quarters(): return jax.lax.all_gather(local_values, ax_name).sum(axis=0)]
where the time goes in v1:
time: 668 us; the launch traced here: 667 us
  waiting for transfers between devices  556 us (83%)
  other arithmetic  77.6 us (12%)
  matrix products  16.7 us (2%)
  between operations  13.4 us (2%)
    all_gather x1, waiting for transfers between devices, carried_in(): gathered = lax.all_gather(value.astype(jnp.bfloat16), axis)  288 us
    all_gather x2, waiting for transfers between devices, _begin_quarters(): return jax.lax.all_gather(local_values, ax_name).sum(axis=0)  268 us
    add x15, other arithmetic, add_terms(): return earlier + later  32.7 us
    reduce_sum x2, other arithmetic, _begin_quarters(): return jax.lax.all_gather(local_values, ax_name).sum(axis=0)  27.7 us
  transfers between devices with their start and end apart: 3, of which 3 were waited for; matrix products, arithmetic and copies ran while one was open for 0% of the time, Pallas kernels for 0%

profile of v1, /device:TPU:248, one launch (start us, length us, event | category | flops | bytes accessed | tf_op | source)
XLA Modules:
  0.0 667.1 jit_solution(7750291460850466948)
XLA Ops:
  6.5 0.0 copy-start
  6.5 0.0 all-gather.5.cloned.1.call-start
  6.5 2.2 convert_element_type.68
  8.7 0.7 fusion.38
  9.5 0.0 copy-start.11
  9.5 0.0 copy-start.7
  9.5 0.7 fusion.39
  10.3 0.4 copy-done.7
  10.7 0.7 fusion.40
  11.5 1.2 fusion.21
  12.7 1.4 fusion.20
  14.1 1.1 fusion.25
  15.3 1.4 pad_maximum_fusion
  16.6 0.0 all-gather.5.cloned.1.call-update
  16.7 0.0 all-gather.7.cloned.1.call-start
  16.7 133.8 %all-gather.5.cloned.1.call-done = bf16[16,3,512,512]{3,2,1,0:T(8,128)(2,1)} async-done(((bf16[1,3,512,512]{3,2,1,0:T(8,128)(2,1)}), bf16[16,3,512,512]{3,2,1,0:T(8,128)(2,1)}) %all-gather.5.cloned.1.call-update) | async-done | bytes 25165840 | tf_op jit(solution)/shard_map/all_gather | solution.py:9
  150.6 13.2 %reduce_sum.60 = bf16[3,512,512]{2,1,0:T(8,128)(2,1)S(1)} reduce(bf16[16,3,512,512]{3,2,1,0:T(8,128)(2,1)} %all-gather.5.cloned.1.call-done, bf16[]{:T(256)} %constant.27.clone.1), dimensions={0}, to_apply=%region_0.0 | reduce | flops 11796480 | bytes 26738690 | tf_op jit(solution)/shard_map/reduce_sum | solution.py:9
  163.7 0.0 copy-start.4
  163.8 0.0 copy-start.2
  163.8 3.2 multiply_reduce_fusion.3
  167.0 0.2 copy-done.2
  167.2 0.4 multiply_convert_fusion.1
  167.6 0.7 fusion.35
  168.3 0.0 copy-done.4
  168.3 0.0 copy-start.8
  168.3 0.7 fusion.36
  169.1 0.5 copy-done.8
  169.5 0.7 fusion.37
  170.3 1.2 fusion.24
  171.5 1.4 fusion.22
  172.9 1.2 fusion.23
  174.1 1.3 pad_maximum_fusion.1
  175.5 0.0 all-gather.7.cloned.1.call-update
  175.5 0.2 all-gather.9.cloned.1.call-start
  175.7 134.2 %all-gather.7.cloned.1.call-done = bf16[16,3,512,512]{3,2,1,0:T(8,128)(2,1)} async-done(((bf16[1,3,512,512]{3,2,1,0:T(8,128)(2,1)}), bf16[16,3,512,512]{3,2,1,0:T(8,128)(2,1)}) %all-gather.7.cloned.1.call-update) | async-done | bytes 25165840 | tf_op jit(solution)/shard_map/all_gather | solution.py:9
  310.0 14.5 %reduce_sum.63 = bf16[3,512,512]{2,1,0:T(8,128)(2,1)} reduce(bf16[16,3,512,512]{3,2,1,0:T(8,128)(2,1)} %all-gather.7.cloned.1.call-done, bf16[]{:T(256)} %constant.27.clone.1), dimensions={0}, to_apply=%region_3.0 | reduce | flops 11796480 | bytes 26738690 | tf_op jit(solution)/shard_map/reduce_sum | solution.py:9
  324.4 3.0 multiply_reduce_fusion.1
  327.5 1.8 fusion
  329.3 0.0 all-gather.9.cloned.1.call-update
  329.3 287.9 %all-gather.9.cloned.1.call-done = bf16[48,512,512]{2,1,0:T(8,128)(2,1)} async-done(((bf16[3,512,512]{2,1,0:T(8,128)(2,1)}), bf16[48,512,512]{2,1,0:T(8,128)(2,1)}) %all-gather.9.cloned.1.call-update) | async-done | bytes 25165840 | tf_op jit(solution)/shard_map/all_gather | solution.py:17
  617.2 0.4 broadcast_in_dim.2
  617.6 33.1 %while.10 = (s32[]{:T(128)}, f32[3,512,512]{2,1,0:T(8,128)S(1)}, s32[]{:T(128)}, bf16[16,3,512,512]{3,2,1,0:T(8,128)(2,1)}, s32[]{:T(128)}, /*index=5*/s32[]{:T(128)}, s32[]{:T(128)}) while((s32[]{:T(128)}, f32[3,512,512]{2,1,0:T(8,128)S(1)}, s32[]{:T(128)}, bf16[16,3,512,512]{3,2,1,0:T(8,128)(2,1)}, s32[]{:T(128)}, /*index=5*/s32[]{:T(128)}, ...), condition=%wide.region_6.7_spmd, body=%wide.region_5.6_spmd.sunk | while | flops 1572869 | bytes 7864443 | solution.py:23
  617.6 2.2 convert_add_fusion.2
  619.8 2.2 convert_add_fusion.2
  622.0 2.2 convert_add_fusion.2
  624.2 2.2 convert_add_fusion.2
  626.4 2.2 convert_add_fusion.2
  628.6 2.2 convert_add_fusion.2
  630.9 2.2 convert_add_fusion.2
  633.1 2.2 convert_add_fusion.2
  635.3 2.2 convert_add_fusion.2
  637.5 2.2 convert_add_fusion.2
  639.7 2.2 convert_add_fusion.2
  641.9 2.2 convert_add_fusion.2
  644.1 2.2 convert_add_fusion.2
  646.3 2.2 convert_add_fusion.2
  648.5 2.2 convert_add_fusion.2
  650.7 3.6 multiply_reduce_fusion
  654.4 0.0 copy-start.10
  654.4 0.3 multiply_convert_fusion
  654.7 1.1 copy-done.9
  655.8 0.7 fusion.34
  656.6 0.0 copy-start.1
  656.6 3.9 convolution_convert_fusion
  (16 shorter events, 0.1 us)
Async XLA Ops:
  6.5 2.2 copy-start
  6.5 144.0 %all-gather.5.cloned.1.call-start = ((), (), s32[]{:S(2)}) async-start(), calls=%async_computation | async-start | bytes 26738688 | tf_op jit(solution)/shard_map/all_gather | solution.py:9
  9.5 0.8 copy-start.11
  9.5 1.2 copy-start.7
  16.7 293.3 %all-gather.7.cloned.1.call-start = ((), (), s32[]{:S(2)}) async-start(), calls=%async_computation.1 | async-start | bytes 26738688 | tf_op jit(solution)/shard_map/all_gather | solution.py:9
  163.7 4.6 copy-start.4
  163.8 3.4 copy-start.2
  168.3 1.2 copy-start.8
  175.5 441.7 %all-gather.9.cloned.1.call-start = ((), (), s32[]{:S(2)}) async-start(), calls=%async_computation.2 | async-start | bytes 26738688 | tf_op jit(solution)/shard_map/all_gather | solution.py:17
  310.0 14.5 %copy-start.3 = (f32[3,512,512]{2,1,0:T(8,128)S(1)}, f32[3,512,512]{2,1,0:T(8,128)}, u32[]{:S(2)}) copy-start(f32[3,512,512]{2,1,0:T(8,128)} %param.11) | copy-start | bytes 9437188
  324.4 3.0 copy-start.5
  324.4 3.0 copy-start.6
  654.4 1.4 copy-start.10
  654.7 1.1 copy-start.9
  656.6 4.0 copy-start.1
Sparse Core Ops, SparseCore 0:
  16.8 133.7 all-gather.4
  175.6 134.3 all-gather.6
  329.4 287.7 all-gather.8
